TPU v7x, 32 devices: a whole 2x2x4 slice. The times are simulated.
32 devices in a mesh: req: 4 (over y, x), head: 8 (over z, core).
Axes of the slice: x: 2, y: 2, z: 4, core: 2. Of those that a mesh axis runs over, the one named last changes fastest.
Arguments:
- hidden: bfloat16 [4, 256, 5120], P('req', 'head'), may hold values from -6 to 6
- cached_len: int32 [4], P('req'), may hold values from 2 to 4096, as said below
- attn_gain: float32 [5120], replicated, may hold values from 0.5 to 1.5
- query_key_value_weight: bfloat16 [5120, 6144], P(None, 'head'), may hold values from -0.078125 to 0.078125
- b_qkv: bfloat16 [6144], P('head'), may hold values from -1.5 to 1.5
- key_cache: bfloat16 [4, 4096, 1024], P('req', 'head'), may hold values from -4000 to 4000
- value_cache: bfloat16 [4, 4096, 1024], P('req', 'head'), may hold values from -6 to 6
- w_out: bfloat16 [4096, 5120], P('head'), may hold values from -0.09375 to 0.09375
- ffn_gain: float32 [5120], replicated, may hold values from 0.5 to 1.5
- w_gate: bfloat16 [5120, 13824], P(None, 'head'), may hold values from -0.078125 to 0.078125
- w_up: bfloat16 [5120, 13824], P(None, 'head'), may hold values from -0.078125 to 0.078125
- w_down: bfloat16 [13824, 5120], P('head'), may hold values from -0.0546875 to 0.0546875
Outputs:
- layer_out: bfloat16 [4, 256, 5120], P('req', 'head')
- new_keys: bfloat16 [4, 256, 1024], P('req', 'head')
- new_values: bfloat16 [4, 256, 1024], P('req', 'head')
Inputs may be any that keep to these rules, and one draw needn't show every extreme that they name: `cached_len`: about half of the requests have nearly full caches, within 512 of 4096, one of them exactly 4096; the others hold fewer than 512 positions; which requests are which is drawn.
All inputs are finite; a program needn't handle non-finite values.
Results may differ from a plain program's by a relative error of at most 0.015.
Values may be sent and summed in bfloat16 or wider, within the bound.
A program may use at most 256 MiB of HBM per device.

v0:
```python
import math
import jax
import jax.numpy as jnp
from jax import lax
from jax.sharding import PartitionSpec as P

QUERY_HEADS = 32
KEY_VALUE_HEADS = 8
HEAD_WIDTH = 128
rope_base = 1000000.0


def rms_norm(values, gain):
    data = values.astype(jnp.float32)
    spread = jnp.mean(data * data, axis=-1, keepdims=True)
    return (data * lax.rsqrt(spread + 1e-06) * gain).astype(jnp.bfloat16)


def rope_apply(values, positions):
    half_dim = HEAD_WIDTH // 2
    inverse = rope_base ** (-(jnp.arange(half_dim, dtype=jnp.float32) * 2.0 / HEAD_WIDTH))
    angles = positions.astype(jnp.float32)[:, None] * inverse[None, :]
    cosine = jnp.concatenate([jnp.cos(angles), jnp.cos(angles)], axis=-1)[:, None, :]
    sine = jnp.concatenate([jnp.sin(angles), jnp.sin(angles)], axis=-1)[:, None, :]
    data = values.astype(jnp.float32)
    rotated = jnp.concatenate([-data[..., half_dim:], data[..., :half_dim]], axis=-1)
    return (data * cosine + rotated * sine).astype(jnp.bfloat16)


def on_device(
    hidden,
    cached_len,
    attn_gain,
    query_key_value_weight,
    b_qkv,
    key_cache,
    value_cache,
    w_out,
    ffn_gain,
    w_gate,
    w_up,
    w_down,
):
    group_size = lax.axis_size("head")
    index_here = lax.axis_index("head")
    own_rows = hidden[0]
    fresh_count = own_rows.shape[0]
    all_rows = lax.all_gather(own_rows, "head", axis=0, tiled=True)
    token_total = all_rows.shape[0]
    head_group = QUERY_HEADS // KEY_VALUE_HEADS
    heads_here = QUERY_HEADS // group_size
    scale = 1.0 / math.sqrt(HEAD_WIDTH)
    normed = rms_norm(all_rows, attn_gain)
    qkv_part = (
        jnp.dot(normed, query_key_value_weight, preferred_element_type=jnp.float32)
        + b_qkv.astype(jnp.float32)
    ).astype(jnp.bfloat16)
    query_key_value = lax.all_gather(qkv_part, "head", axis=1, tiled=True)
    query_rows = query_key_value[:, : QUERY_HEADS * HEAD_WIDTH].reshape(
        token_total, QUERY_HEADS, HEAD_WIDTH
    )
    fresh_keys = query_key_value[
        :, QUERY_HEADS * HEAD_WIDTH : (QUERY_HEADS + KEY_VALUE_HEADS) * HEAD_WIDTH
    ].reshape(token_total, KEY_VALUE_HEADS, HEAD_WIDTH)
    fresh_values = query_key_value[:, (QUERY_HEADS + KEY_VALUE_HEADS) * HEAD_WIDTH :].reshape(
        token_total, KEY_VALUE_HEADS, HEAD_WIDTH
    )
    token_ids = jnp.arange(token_total, dtype=jnp.int32)
    positions = cached_len[0] + token_ids
    query_rows = rope_apply(query_rows, positions)
    fresh_keys = rope_apply(fresh_keys, positions)
    row_start = index_here * fresh_count
    request_keys = lax.dynamic_slice_in_dim(fresh_keys, row_start, fresh_count, 0)
    request_values = lax.dynamic_slice_in_dim(fresh_values, row_start, fresh_count, 0)
    key_lines = request_keys.reshape(1, fresh_count, KEY_VALUE_HEADS * HEAD_WIDTH)
    value_lines = request_values.reshape(1, fresh_count, KEY_VALUE_HEADS * HEAD_WIDTH)
    cache_length = key_cache.shape[1]
    joined_keys = jnp.concatenate(
        [key_cache[0].reshape(cache_length, KEY_VALUE_HEADS, HEAD_WIDTH), request_keys], axis=0
    )
    joined_values = jnp.concatenate(
        [value_cache[0].reshape(cache_length, KEY_VALUE_HEADS, HEAD_WIDTH), request_values], axis=0
    )
    cache_ok = index_here * cache_length + jnp.arange(cache_length, dtype=jnp.int32) < cached_len[0]
    own_ids = row_start + jnp.arange(fresh_count, dtype=jnp.int32)
    new_ok = own_ids[None, :] <= token_ids[:, None]
    allowed = jnp.concatenate(
        [jnp.broadcast_to(cache_ok[None, :], (token_total, cache_length)), new_ok], axis=1
    )
    grouped_queries = query_rows.reshape(token_total, KEY_VALUE_HEADS, head_group, HEAD_WIDTH)
    scores = (
        jnp.einsum(
            "tkjd,skd->kjts", grouped_queries, joined_keys, preferred_element_type=jnp.float32
        )
        * scale
    )
    scores = jnp.where(allowed[None, None], scores, -1e30)
    row_max = jnp.max(scores, axis=-1)
    expo = jnp.where(allowed[None, None], jnp.exp(scores - row_max[..., None]), 0.0)
    row_sum = jnp.sum(expo, axis=-1)
    weights = expo.astype(jnp.bfloat16)
    weighted = jnp.einsum(
        "kjts,skd->tkjd", weights, joined_values, preferred_element_type=jnp.float32
    )
    weighted = weighted.reshape(token_total, QUERY_HEADS, HEAD_WIDTH)
    row_max = jnp.transpose(row_max, (2, 0, 1)).reshape(token_total, QUERY_HEADS)
    row_sum = jnp.transpose(row_sum, (2, 0, 1)).reshape(token_total, QUERY_HEADS)
    sums_got, max_got, total_got = (
        lax.all_to_all(
            weighted[None].astype(jnp.bfloat16), "head", split_axis=2, concat_axis=0, tiled=True
        ).astype(jnp.float32),
        lax.all_to_all(
            row_max[None].astype(jnp.bfloat16), "head", split_axis=2, concat_axis=0, tiled=True
        ).astype(jnp.float32),
        lax.all_to_all(
            row_sum[None].astype(jnp.bfloat16), "head", split_axis=2, concat_axis=0, tiled=True
        ).astype(jnp.float32),
    )
    joint = jnp.max(max_got, axis=0)
    factor = jnp.exp(max_got - joint[None])
    total_here = jnp.sum(total_got * factor, axis=0)
    sums_here = jnp.sum(sums_got * factor[..., None], axis=0)
    attn = (
        (sums_here / total_here[..., None])
        .astype(jnp.bfloat16)
        .reshape(token_total, heads_here * HEAD_WIDTH)
    )
    projected = jnp.dot(attn, w_out, preferred_element_type=jnp.float32)
    projected = lax.psum(projected.astype(jnp.bfloat16), "head").astype(jnp.float32)
    middle = (all_rows.astype(jnp.float32) + projected).astype(jnp.bfloat16)
    normed_two = rms_norm(middle, ffn_gain)
    middle_own = lax.dynamic_slice_in_dim(middle, row_start, fresh_count, 0)
    gate = jnp.dot(normed_two, w_gate, preferred_element_type=jnp.float32)
    upward = jnp.dot(normed_two, w_up, preferred_element_type=jnp.float32)
    active = (jax.nn.silu(gate) * upward).astype(jnp.bfloat16)
    ffn_part = lax.psum_scatter(
        jnp.dot(active, w_down, preferred_element_type=jnp.float32).astype(jnp.bfloat16),
        "head",
        scatter_dimension=0,
        tiled=True,
    ).astype(jnp.float32)
    result = (middle_own.astype(jnp.float32) + ffn_part).astype(jnp.bfloat16)
    return (result[None], key_lines, value_lines)


def solution(mesh):
    in_specs = (
        P("req", "head", None),
        P("req"),
        P(),
        P(None, "head"),
        P("head"),
        P("req", "head", None),
        P("req", "head", None),
        P("head", None),
        P(),
        P(None, "head"),
        P(None, "head"),
        P("head", None),
    )
    out_specs = (P("req", "head", None), P("req", "head", None), P("req", "head", None))
    return jax.shard_map(
        on_device, mesh=mesh, in_specs=in_specs, out_specs=out_specs, check_vma=False
    )
```

profile of v0, /device:TPU:0, one launch (start us, length us, event | category | flops | bytes accessed | tf_op | source)
XLA Modules:
  0.0 385.5 jit_solution(16978504178929794533)
XLA Ops:
  8.6 37.6 %all-gather.6.cloned.1.call-done = bf16[1,256,5120]{2,1,0:T(8,128)(2,1)} async-done(((bf16[1,32,5120]{2,1,0:T(8,128)(2,1)}), bf16[1,256,5120]{2,1,0:T(8,128)(2,1)}) %all-gather.6.cloned.1.call-update) | async-done | bytes 2621456 | tf_op jit(solution)/shard_map/all_gather | solution.py:48
  46.3 2.3 fusion.9
  48.6 7.1 %fusion.32 = bf16[256,768]{1,0:T(8,128)(2,1)} fusion(bf16[5120,768]{1,0:T(8,128)(2,1)} %param.15, bf16[1,256,5120]{2,1,0:T(8,128)(2,1)} %all-gather.6.cloned.1.call-done, f32[5120]{0:T(1024)} %param.14, f32[256]{0:T(256)S(1)} %add_rsqrt_fusion.1, f32[768]{0:T(1024)S(1)} %convert_element_type.173), kind=kOutput, calls=%fused_computation.40 | convolution fusion | flops 2018902016 | bytes 10903552 | tf_op jit(solution)/shard_map/dot_general | solution.py:55
  62.4 30.8 %all-gather.4.cloned.1.call-done = bf16[256,6144]{1,0:T(8,128)(2,1)} async-done(((bf16[256,768]{1,0:T(8,128)(2,1)}), bf16[256,6144]{1,0:T(8,128)(2,1)}) %all-gather.4.cloned.1.call-update) | async-done | bytes 3145744 | tf_op jit(solution)/shard_map/all_gather | solution.py:58
  93.2 2.3 slice_bitcast_fusion
  96.7 2.5 slice_convert_fusion
  99.1 5.6 %copy.75 = f32[256,4096]{0,1:T(8,128)} copy(f32[256,4096]{1,0:T(8,128)} %slice_convert_fusion) | data formatting | bytes 8388608 | tf_op jit(solution)/shard_map/convert_element_type | solution.py:25
  104.7 6.0 %reshape.139 = f32[256,8,4,128]{3,2,1,0:T(4,128)} reshape(f32[256,4096]{1,0:T(8,128)} %slice_convert_fusion) | data formatting | bytes 8388608 | tf_op jit(solution)/shard_map/convert_element_type | solution.py:25
  115.1 3.8 copy.76
  118.9 2.8 copy.77
  122.8 13.2 %fusion = (f32[8,4,256]{2,1,0:T(4,128)S(1)}, f32[8,544,256,4]{2,1,3,0:T(8,128)}) fusion(pred[256,544]{0,1:T(8,128)(4,1)S(1)} %pad_add_fusion, f32[256,8,4,64]{3,0,2,1:T(8,128)} %copy.77, f32[256,8,4,64]{3,0,2,1:T(8,128)} %copy.76, f32[256,8,4,128]{3,2,1,0:T(4,128)} %reshape.139, f32[256,128]{1,0:T(8,128)S(1)} %get-tuple-element.18, ...), kind=kOutput, calls=%fused_computation.2 | convolution fusion | flops 1161682944 | bytes 27762688 | tf_op jit(solution)/shard_map/tkjd,skd->kjts/dot_general | solution.py:92
  136.1 10.5 %fusion.1 = bf16[8,4,256]{2,1,0:T(4,128)(2,1)S(1)} fusion(f32[8,544,256,4]{2,1,3,0:T(8,128)} %get-tuple-element.16, f32[8,4,256]{2,1,0:T(4,128)S(1)} %get-tuple-element.15, pred[256,544]{0,1:T(8,128)(4,1)S(1)} %pad_add_fusion), kind=kLoop, calls=%fused_computation.3 | loop fusion | flops 22274048 | bytes 18014208 | tf_op jit(solution)/shard_map/reduce_sum | solution.py:100
  148.5 3.3 all-to-all-start.2
  153.3 4.1 %all-to-all-done.2 = bf16[8,2,512]{2,1,0:T(2,128)(2,1)S(1)} async-done(((bf16[8,2,512]{2,1,0:T(2,128)(2,1)}), bf16[8,2,512]{2,1,0:T(2,128)(2,1)S(1)}, u32[]{:S(2)}, u32[]{:S(2)}) %all-to-all-start.2) | async-done | bytes 16416 | tf_op jit(solution)/shard_map/all_to_all | solution.py:115
  157.4 3.3 all-to-all-start.1
  160.7 9.4 %fusion.26 = bf16[8,128,4,256]{3,1,2,0:T(8,128)(2,1)} fusion(f32[8,544,256,4]{2,1,3,0:T(8,128)} %get-tuple-element.16, f32[8,4,256]{2,1,0:T(4,128)S(1)} %get-tuple-element.15, pred[256,544]{0,1:T(8,128)(4,1)S(1)} %pad_add_fusion, bf16[32,8,128]{2,0,1:T(8,128)(2,1)S(1)} %copy.87, bf16[512,8,128]{2,0,1:T(8,128)(2,1)S(1)} %copy-done.7), kind=kOutput, calls=%fused_computation.38 | convolution fusion | flops 1166409728 | bytes 21209088 | tf_op jit(solution)/shard_map/kjts,skd->tkjd/dot_general | solution.py:102
  170.2 5.0 %all-to-all-start = ((bf16[1,256,32,128]{1,3,0,2:T(8,128)(2,1)}), bf16[1,256,32,128]{1,3,0,2:T(8,128)(2,1)S(1)}, u32[]{:S(2)}, u32[]{:S(2)}) async-start(bf16[1,256,32,128]{1,3,0,2:T(8,128)(2,1)} %bitcast.122), calls=%async_computation | async-start | bytes 4194304 | tf_op jit(solution)/shard_map/all_to_all | solution.py:109
  175.6 48.7 %all-to-all-done = bf16[1,256,32,128]{1,3,0,2:T(8,128)(2,1)S(1)} async-done(((bf16[1,256,32,128]{1,3,0,2:T(8,128)(2,1)}), bf16[1,256,32,128]{1,3,0,2:T(8,128)(2,1)S(1)}, u32[]{:S(2)}, u32[]{:S(2)}) %all-to-all-start) | async-done | bytes 2097184 | tf_op jit(solution)/shard_map/all_to_all | solution.py:109
  224.7 5.7 %convolution_convert_fusion.1 = bf16[256,5120]{1,0:T(8,128)(2,1)} fusion(bf16[256,512]{0,1:T(8,128)(2,1)S(1)} %bitcast.123, bf16[512,5120]{1,0:T(8,128)(2,1)} %param.19), kind=kOutput, calls=%fused_computation.13 | convolution fusion | flops 1343488000 | bytes 8126464 | tf_op jit(solution)/shard_map/dot_general | solution.py:128
  230.5 68.1 %all-reduce.2.cloned.1.call-done = bf16[256,5120]{1,0:T(8,128)(2,1)} async-done(((bf16[256,5120]{1,0:T(8,128)(2,1)}), bf16[256,5120]{1,0:T(8,128)(2,1)}) %all-reduce.2.cloned.1.call-update) | async-done | bytes 2621456 | tf_op jit(solution)/shard_map/psum | solution.py:129
  298.7 2.9 fusion.6
  303.1 8.9 %fusion.40 = f32[256,1728]{0,1:T(8,128)S(1)} fusion(bf16[5120,1728]{0,1:T(8,128)(2,1)} %param.21, bf16[256,5120]{1,0:T(8,128)(2,1)S(1)} %get-tuple-element.4, f32[5120]{0:T(1024)S(1)} %copy-done.10, f32[256]{0:T(256)S(1)} %add_rsqrt_fusion), kind=kOutput, calls=%fused_computation.51 | convolution fusion | flops 4535091200 | bytes 22107136 | tf_op jit(solution)/shard_map/dot_general | solution.py:133
  312.0 28.5 %convolution_convert_fusion = bf16[256,5120]{1,0:T(8,128)(2,1)} fusion(bf16[1728,5120]{1,0:T(8,128)(2,1)} %param.23, bf16[5120,1728]{0,1:T(8,128)(2,1)} %param.22, f32[256,1728]{0,1:T(8,128)S(1)} %fusion.40, bf16[256,5120]{1,0:T(8,128)(2,1)} %copy-done.2, f32[5120]{0:T(1024)S(1)} %copy-done.10, f32[256]{0:T(256)S(1)} %add_rsqrt_fusion), kind=kOutput, calls=%fused_computation.12 | convolution fusion | flops 9068904448 | bytes 42423296 | tf_op jit(solution)/shard_map/dot_general | solution.py:137
  341.9 35.2 %reduce-scatter.2.cloned.1.call-done = bf16[32,5120]{1,0:T(8,128)(2,1)} async-done(((bf16[256,5120]{1,0:T(8,128)(2,1)}), bf16[32,5120]{1,0:T(8,128)(2,1)}) %reduce-scatter.2.cloned.1.call-update) | async-done | bytes 327696 | tf_op jit(solution)/shard_map/reduce_scatter | solution.py:136
  (82 shorter events, 22.9 us)
Async XLA Ops:
  7.2 39.1 %all-gather.6.cloned.1.call-start = ((), (), s32[]{:S(2)}) async-start(), calls=%async_computation.7 | async-start | bytes 2949120 | tf_op jit(solution)/shard_map/all_gather | solution.py:48
  7.9 85.3 %all-gather.4.cloned.1.call-start = ((), (), s32[]{:S(2)}) async-start(), calls=%async_computation.4 | async-start | bytes 3538944 | tf_op jit(solution)/shard_map/all_gather | solution.py:58
  48.6 7.9 %copy-start.5 = (bf16[1,512,1024]{2,1,0:T(8,128)(2,1)S(1)}, bf16[1,512,1024]{2,1,0:T(8,128)(2,1)}, u32[]{:S(2)}) copy-start(bf16[1,512,1024]{2,1,0:T(8,128)(2,1)} %param.17) | copy-start | bytes 3145732
  55.7 2.6 copy-start.6
  93.2 3.5 copy-start.3
  110.8 2.6 copy-start
  122.8 13.2 %copy-start.8 = (bf16[32,8,128]{2,0,1:T(8,128)(2,1)}, bf16[32,8,128]{2,0,1:T(8,128)(2,1)S(1)}, u32[]{:S(2)}) copy-start(bf16[32,8,128]{2,0,1:T(8,128)(2,1)S(1)} %fusion.46) | copy-start | bytes 196612
  136.1 15.7 %copy-start.4 = (bf16[32,8,8,128]{3,1,2,0:T(8,128)(2,1)S(1)}, bf16[32,8,8,128]{3,1,2,0:T(8,128)(2,1)}, u32[]{:S(2)}) copy-start(bf16[32,8,8,128]{3,1,2,0:T(8,128)(2,1)} %get-tuple-element.7) | copy-start | bytes 1572868
  136.1 24.6 %copy-start.7 = (bf16[512,8,128]{2,0,1:T(8,128)(2,1)S(1)}, bf16[512,8,128]{2,0,1:T(8,128)(2,1)}, u32[]{:S(2)}) copy-start(bf16[512,8,128]{2,0,1:T(8,128)(2,1)} %copy.68) | copy-start | bytes 3145732
  148.5 8.9 %all-to-all-start.2 = ((bf16[8,2,512]{2,1,0:T(2,128)(2,1)}), bf16[8,2,512]{2,1,0:T(2,128)(2,1)S(1)}, u32[]{:S(2)}, u32[]{:S(2)}) async-start(bf16[8,2,512]{2,1,0:T(2,128)(2,1)} %reshape.155), calls=%async_computation.2 | async-start | bytes 32768 | tf_op jit(solution)/shard_map/all_to_all | solution.py:115
  157.4 12.8 %all-to-all-start.1 = ((bf16[8,2,512]{2,1,0:T(2,128)(2,1)}), bf16[8,2,512]{2,1,0:T(2,128)(2,1)S(1)}, u32[]{:S(2)}, u32[]{:S(2)}) async-start(bf16[8,2,512]{2,1,0:T(2,128)(2,1)} %reshape.153), calls=%async_computation.1 | async-start | bytes 32768 | tf_op jit(solution)/shard_map/all_to_all | solution.py:112
  170.2 54.1 %all-to-all-start = ((bf16[1,256,32,128]{1,3,0,2:T(8,128)(2,1)}), bf16[1,256,32,128]{1,3,0,2:T(8,128)(2,1)S(1)}, u32[]{:S(2)}, u32[]{:S(2)}) async-start(bf16[1,256,32,128]{1,3,0,2:T(8,128)(2,1)} %bitcast.122), calls=%async_computation | async-start | bytes 4194304 | tf_op jit(solution)/shard_map/all_to_all | solution.py:109
  175.2 123.5 %all-reduce.2.cloned.1.call-start = ((), (), s32[]{:S(2)}) async-start(), calls=%async_computation.5 | async-start | bytes 5242880 | tf_op jit(solution)/shard_map/psum | solution.py:129
  224.7 74.0 %copy-start.1 = (bf16[1,256,5120]{2,1,0:T(8,128)(2,1)S(1)}, bf16[1,256,5120]{2,1,0:T(8,128)(2,1)}, u32[]{:S(2)}) copy-start(bf16[1,256,5120]{2,1,0:T(8,128)(2,1)} %all-gather.6.cloned.1.call-done) | copy-start | bytes 7864324
  230.5 72.7 %copy-start.10 = (f32[5120]{0:T(1024)S(1)}, f32[5120]{0:T(1024)}, u32[]{:S(2)}) copy-start(f32[5120]{0:T(1024)} %param.20) | copy-start | bytes 61444
  230.5 146.6 %reduce-scatter.2.cloned.1.call-start = ((), (), s32[]{:S(2)}) async-start(), calls=%async_computation.6 | async-start | bytes 2949120 | tf_op jit(solution)/shard_map/reduce_scatter | solution.py:136
  301.6 1.5 copy-start.2
  312.0 28.5 %copy-start.9 = (bf16[32,8,128]{2,0,1:T(8,128)(2,1)S(1)}, bf16[32,8,128]{2,0,1:T(8,128)(2,1)}, u32[]{:S(2)}) copy-start(bf16[32,8,128]{2,0,1:T(8,128)(2,1)} %copy-done.8) | copy-start | bytes 196612
Sparse Core Ops, SparseCore 0:
  9.6 36.5 all-gather.5
  55.9 37.2 all-gather.3
  230.6 68.0 all-reduce.1
  340.6 36.4 reduce-scatter.1
where the time goes:
time: 386 us; the launch traced here: 385 us
  waiting for transfers between devices  225 us (58%)
  matrix products  72.8 us (19%)
  local copies, waits for them, and re-layouts  30.7 us (8%)
  other arithmetic  30.1 us (8%)
  between operations  14.8 us (4%)
  starting transfers between devices  11.8 us (3%)
    psum x1, waiting for transfers between devices, on_device(): lax.psum(projected.astype(jnp.bfloat16), 'head').astype(jnp.float32)  68.1 us
    all_to_all x1, waiting for transfers between devices, on_device(): lax.all_to_all(weighted[None].astype(jnp.bfloat16), 'head', split_axis=2,...  48.7 us
    all_gather x1, waiting for transfers between devices, on_device(): all_rows = lax.all_gather(own_rows, 'head', axis=0, tiled=True)  37.6 us
    reduce_scatter x1, waiting for transfers between devices, on_device(): lax.psum_scatter(jnp.dot(active, w_down, preferred_element_type=jnp.float...  35.2 us
    all_gather x1, waiting for transfers between devices, on_device(): query_key_value = lax.all_gather(qkv_part, 'head', axis=1, tiled=True)  30.8 us
    dot_general x1, matrix products, on_device(): jnp.dot(active, w_down, preferred_element_type=jnp.float32)  28.5 us
    dot_general x1, matrix products, on_device(): jnp.einsum('tkjd,skd->kjts', grouped_queries, joined_keys, preferred_elem...  13.2 us
    convert_element_type x2, local copies, waits for them, and re-layouts, rope_apply(): data = values.astype(jnp.float32)  11.6 us
  transfers between devices with their start and end apart: 7, of which 6 were waited for; matrix products, arithmetic and copies ran while one was open for 5% of the time, Pallas kernels for 0%

commit v1 on v0

--- a/solution.py
+++ b/solution.py
@@ -106,8 +106,16 @@
     row_max = jnp.transpose(row_max, (2, 0, 1)).reshape(token_total, QUERY_HEADS)
     row_sum = jnp.transpose(row_sum, (2, 0, 1)).reshape(token_total, QUERY_HEADS)
     sums_got, max_got, total_got = (
-        lax.all_to_all(
-            weighted[None].astype(jnp.bfloat16), "head", split_axis=2, concat_axis=0, tiled=True
+        jnp.concatenate(
+            lax.all_to_all(
+                jnp.stack(
+                    jnp.split(weighted[None].astype(jnp.bfloat16), lax.axis_size("head"), axis=2)
+                ),
+                "head",
+                0,
+                0,
+            ),
+            axis=0,
         ).astype(jnp.float32),
         lax.all_to_all(
             row_max[None].astype(jnp.bfloat16), "head", split_axis=2, concat_axis=0, tiled=True

time: 386 us -> 388 us (level)
    all_to_all x1, waiting for transfers between devices: 4.05 us -> 0.01 us  [on_device(): lax.all_to_all(row_sum[None].astype(jnp.bfloat16), 'head', split_axis=2,...]
    unnamed x33 -> x44, local copies, waits for them, and re-layouts: 6.07 us -> 8.71 us
where the time goes in v1:
time: 388 us
  waiting for transfers between devices  224 us (58%)
  matrix products  71.8 us (19%)
  local copies, waits for them, and re-layouts  34.3 us (9%)
  other arithmetic  30.1 us (8%)
  between operations  14.9 us (4%)
  starting transfers between devices  12.1 us (3%)
    psum x1, waiting for transfers between devices, on_device(): lax.psum(projected.astype(jnp.bfloat16), 'head').astype(jnp.float32)  68 us
    all_to_all x1, waiting for transfers between devices, on_device(): lax.all_to_all(jnp.stack(jnp.split(weighted[None].astype(jnp.bfloat16), l...  48.6 us
    all_gather x1, waiting for transfers between devices, on_device(): all_rows = lax.all_gather(own_rows, 'head', axis=0, tiled=True)  37.6 us
    reduce_scatter x1, waiting for transfers between devices, on_device(): lax.psum_scatter(jnp.dot(active, w_down, preferred_element_type=jnp.float...  35.3 us
    all_gather x1, waiting for transfers between devices, on_device(): query_key_value = lax.all_gather(qkv_part, 'head', axis=1, tiled=True)  30.8 us
    dot_general x1, matrix products, on_device(): jnp.dot(active, w_down, preferred_element_type=jnp.float32)  28.5 us
    dot_general x1, matrix products, on_device(): jnp.einsum('tkjd,skd->kjts', grouped_queries, joined_keys, preferred_elem...  13.2 us
    convert_element_type x2, local copies, waits for them, and re-layouts, rope_apply(): data = values.astype(jnp.float32)  11.6 us
  transfers between devices with their start and end apart: 7, of which 6 were waited for; matrix products, arithmetic and copies ran while one was open for 5% of the time, Pallas kernels for 0%

profile of v1, /device:TPU:0, one launch (start us, length us, event | category | flops | bytes accessed | tf_op | source)
XLA Modules:
  0.0 387.7 jit_solution(3213616283901316228)
XLA Ops:
  8.6 37.6 %all-gather.6.cloned.1.call-done = bf16[1,256,5120]{2,1,0:T(8,128)(2,1)} async-done(((bf16[1,32,5120]{2,1,0:T(8,128)(2,1)}), bf16[1,256,5120]{2,1,0:T(8,128)(2,1)}) %all-gather.6.cloned.1.call-update) | async-done | bytes 2621456 | tf_op jit(solution)/shard_map/all_gather | solution.py:48
  46.3 2.3 fusion.9
  48.6 7.1 %fusion.32 = bf16[256,768]{1,0:T(8,128)(2,1)} fusion(bf16[5120,768]{1,0:T(8,128)(2,1)} %param.15, bf16[1,256,5120]{2,1,0:T(8,128)(2,1)} %all-gather.6.cloned.1.call-done, f32[5120]{0:T(1024)} %param.14, f32[256]{0:T(256)S(1)} %add_rsqrt_fusion.1, f32[768]{0:T(1024)S(1)} %convert_element_type.167), kind=kOutput, calls=%fused_computation.40 | convolution fusion | flops 2018902016 | bytes 10903552 | tf_op jit(solution)/shard_map/dot_general | solution.py:55
  62.4 30.8 %all-gather.4.cloned.1.call-done = bf16[256,6144]{1,0:T(8,128)(2,1)} async-done(((bf16[256,768]{1,0:T(8,128)(2,1)}), bf16[256,6144]{1,0:T(8,128)(2,1)}) %all-gather.4.cloned.1.call-update) | async-done | bytes 3145744 | tf_op jit(solution)/shard_map/all_gather | solution.py:58
  93.2 2.3 slice_bitcast_fusion
  96.7 2.5 slice_convert_fusion
  99.2 5.6 %copy.102 = f32[256,4096]{0,1:T(8,128)} copy(f32[256,4096]{1,0:T(8,128)} %slice_convert_fusion) | data formatting | bytes 8388608 | tf_op jit(solution)/shard_map/convert_element_type | solution.py:25
  104.8 6.0 %reshape.138 = f32[256,8,4,128]{3,2,1,0:T(4,128)} reshape(f32[256,4096]{1,0:T(8,128)} %slice_convert_fusion) | data formatting | bytes 8388608 | tf_op jit(solution)/shard_map/convert_element_type | solution.py:25
  115.1 3.8 copy.103
  119.0 2.8 copy.104
  122.9 13.2 %fusion = (f32[8,4,256]{2,1,0:T(4,128)S(1)}, f32[8,544,256,4]{2,1,3,0:T(8,128)}) fusion(pred[256,544]{0,1:T(8,128)(4,1)S(1)} %pad_add_fusion, f32[256,8,4,64]{3,0,2,1:T(8,128)} %copy.104, f32[256,8,4,64]{3,0,2,1:T(8,128)} %copy.103, f32[256,8,4,128]{3,2,1,0:T(4,128)} %reshape.138, f32[256,128]{1,0:T(8,128)S(1)} %get-tuple-element.18, ...), kind=kOutput, calls=%fused_computation.2 | convolution fusion | flops 1161682944 | bytes 27762688 | tf_op jit(solution)/shard_map/tkjd,skd->kjts/dot_general | solution.py:92
  136.1 10.5 %fusion.1 = bf16[8,4,256]{2,1,0:T(4,128)(2,1)S(1)} fusion(f32[8,544,256,4]{2,1,3,0:T(8,128)} %get-tuple-element.16, f32[8,4,256]{2,1,0:T(4,128)S(1)} %get-tuple-element.15, pred[256,544]{0,1:T(8,128)(4,1)S(1)} %pad_add_fusion), kind=kLoop, calls=%fused_computation.3 | loop fusion | flops 22274048 | bytes 18014208 | tf_op jit(solution)/shard_map/reduce_sum | solution.py:100
  148.5 3.3 all-to-all-start.2
  152.0 8.4 %fusion.26 = bf16[8,128,4,256]{3,1,2,0:T(8,128)(2,1)S(1)} fusion(f32[8,544,256,4]{2,1,3,0:T(8,128)} %get-tuple-element.16, f32[8,4,256]{2,1,0:T(4,128)S(1)} %get-tuple-element.15, pred[256,544]{0,1:T(8,128)(4,1)S(1)} %pad_add_fusion, bf16[32,8,128]{2,0,1:T(8,128)(2,1)S(1)} %copy.113, bf16[512,8,128]{2,0,1:T(8,128)(2,1)S(1)} %copy-done.9), kind=kOutput, calls=%fused_computation.38 | convolution fusion | flops 1166409728 | bytes 21209088 | tf_op jit(solution)/shard_map/kjts,skd->tkjd/dot_general | solution.py:102
  163.2 5.0 %all-to-all-start.1 = ((bf16[8,2,512]{2,1,0:T(2,128)(2,1)}), bf16[8,2,512]{2,1,0:T(2,128)(2,1)S(1)}, u32[]{:S(2)}, u32[]{:S(2)}) async-start(bf16[8,2,512]{2,1,0:T(2,128)(2,1)} %reshape.151), calls=%async_computation.1 | async-start | bytes 32768 | tf_op jit(solution)/shard_map/all_to_all | solution.py:120
  170.5 3.3 all-to-all-done.1
  173.9 3.6 all-to-all-start
  177.9 48.6 %all-to-all-done = bf16[8,1,256,4,128]{2,4,3,1,0:T(8,128)(2,1)S(1)} async-done(((bf16[8,1,256,4,128]{2,4,3,1,0:T(8,128)(2,1)}), bf16[8,1,256,4,128]{2,4,3,1,0:T(8,128)(2,1)S(1)}, u32[]{:S(2)}, u32[]{:S(2)}) %all-to-all-start) | async-done | bytes 2097184 | tf_op jit(solution)/shard_map/all_to_all | solution.py:110
  226.9 5.7 %convolution_convert_fusion.1 = bf16[256,5120]{1,0:T(8,128)(2,1)} fusion(bf16[256,512]{0,1:T(8,128)(2,1)S(1)} %bitcast.154, bf16[512,5120]{1,0:T(8,128)(2,1)} %param.19), kind=kOutput, calls=%fused_computation.13 | convolution fusion | flops 1343488000 | bytes 8126464 | tf_op jit(solution)/shard_map/dot_general | solution.py:136
  232.7 68.0 %all-reduce.2.cloned.1.call-done = bf16[256,5120]{1,0:T(8,128)(2,1)} async-done(((bf16[256,5120]{1,0:T(8,128)(2,1)}), bf16[256,5120]{1,0:T(8,128)(2,1)}) %all-reduce.2.cloned.1.call-update) | async-done | bytes 2621456 | tf_op jit(solution)/shard_map/psum | solution.py:137
  300.7 2.9 fusion.6
  305.2 8.9 %fusion.40 = f32[256,1728]{0,1:T(8,128)S(1)} fusion(bf16[5120,1728]{0,1:T(8,128)(2,1)} %param.21, bf16[256,5120]{1,0:T(8,128)(2,1)S(1)} %get-tuple-element.4, f32[5120]{0:T(1024)S(1)} %copy-done.12, f32[256]{0:T(256)S(1)} %add_rsqrt_fusion), kind=kOutput, calls=%fused_computation.51 | convolution fusion | flops 4535091200 | bytes 22107136 | tf_op jit(solution)/shard_map/dot_general | solution.py:141
  314.1 28.5 %convolution_convert_fusion = bf16[256,5120]{1,0:T(8,128)(2,1)} fusion(bf16[1728,5120]{1,0:T(8,128)(2,1)} %param.23, bf16[5120,1728]{0,1:T(8,128)(2,1)} %param.22, f32[256,1728]{0,1:T(8,128)S(1)} %fusion.40, bf16[256,5120]{1,0:T(8,128)(2,1)} %copy-done.2, f32[5120]{0:T(1024)S(1)} %copy-done.12, f32[256]{0:T(256)S(1)} %add_rsqrt_fusion), kind=kOutput, calls=%fused_computation.12 | convolution fusion | flops 9068904448 | bytes 42423296 | tf_op jit(solution)/shard_map/dot_general | solution.py:145
  343.9 35.3 %reduce-scatter.2.cloned.1.call-done = bf16[32,5120]{1,0:T(8,128)(2,1)} async-done(((bf16[256,5120]{1,0:T(8,128)(2,1)}), bf16[32,5120]{1,0:T(8,128)(2,1)}) %reduce-scatter.2.cloned.1.call-update) | async-done | bytes 327696 | tf_op jit(solution)/shard_map/reduce_scatter | solution.py:144
  (94 shorter events, 26.6 us)
Async XLA Ops:
  7.2 39.1 %all-gather.6.cloned.1.call-start = ((), (), s32[]{:S(2)}) async-start(), calls=%async_computation.7 | async-start | bytes 2949120 | tf_op jit(solution)/shard_map/all_gather | solution.py:48
  7.9 85.3 %all-gather.4.cloned.1.call-start = ((), (), s32[]{:S(2)}) async-start(), calls=%async_computation.4 | async-start | bytes 3538944 | tf_op jit(solution)/shard_map/all_gather | solution.py:58
  48.6 7.9 %copy-start.7 = (bf16[1,512,1024]{2,1,0:T(8,128)(2,1)S(1)}, bf16[1,512,1024]{2,1,0:T(8,128)(2,1)}, u32[]{:S(2)}) copy-start(bf16[1,512,1024]{2,1,0:T(8,128)(2,1)} %param.17) | copy-start | bytes 3145732
  55.7 2.6 copy-start.8
  93.2 3.5 copy-start.3
  110.8 2.6 copy-start
  122.9 13.2 %copy-start.10 = (bf16[32,8,128]{2,0,1:T(8,128)(2,1)}, bf16[32,8,128]{2,0,1:T(8,128)(2,1)S(1)}, u32[]{:S(2)}) copy-start(bf16[32,8,128]{2,0,1:T(8,128)(2,1)S(1)} %fusion.54) | copy-start | bytes 196612
  136.1 15.7 %copy-start.6 = (bf16[32,8,8,128]{3,1,2,0:T(8,128)(2,1)S(1)}, bf16[32,8,8,128]{3,1,2,0:T(8,128)(2,1)}, u32[]{:S(2)}) copy-start(bf16[32,8,8,128]{3,1,2,0:T(8,128)(2,1)} %get-tuple-element.7) | copy-start | bytes 1572868
  136.1 15.9 %copy-start.9 = (bf16[512,8,128]{2,0,1:T(8,128)(2,1)S(1)}, bf16[512,8,128]{2,0,1:T(8,128)(2,1)}, u32[]{:S(2)}) copy-start(bf16[512,8,128]{2,0,1:T(8,128)(2,1)} %copy.95) | copy-start | bytes 3145732
  148.5 14.7 %all-to-all-start.2 = ((bf16[8,2,512]{2,1,0:T(2,128)(2,1)}), bf16[8,2,512]{2,1,0:T(2,128)(2,1)S(1)}, u32[]{:S(2)}, u32[]{:S(2)}) async-start(bf16[8,2,512]{2,1,0:T(2,128)(2,1)} %reshape.153), calls=%async_computation.2 | async-start | bytes 32768 | tf_op jit(solution)/shard_map/all_to_all | solution.py:123
  160.4 1.3 copy-start.5
  163.2 10.7 %all-to-all-start.1 = ((bf16[8,2,512]{2,1,0:T(2,128)(2,1)}), bf16[8,2,512]{2,1,0:T(2,128)(2,1)S(1)}, u32[]{:S(2)}, u32[]{:S(2)}) async-start(bf16[8,2,512]{2,1,0:T(2,128)(2,1)} %reshape.151), calls=%async_computation.1 | async-start | bytes 32768 | tf_op jit(solution)/shard_map/all_to_all | solution.py:120
  169.2 1.3 copy-start.4
  173.9 52.6 %all-to-all-start = ((bf16[8,1,256,4,128]{2,4,3,1,0:T(8,128)(2,1)}), bf16[8,1,256,4,128]{2,4,3,1,0:T(8,128)(2,1)S(1)}, u32[]{:S(2)}, u32[]{:S(2)}) async-start(bf16[8,1,256,4,128]{2,4,3,1,0:T(8,128)(2,1)} %copy-done.4), calls=%async_computation | async-start | bytes 4194304 | tf_op jit(solution)/shard_map/all_to_all | solution.py:110
  177.5 123.3 %all-reduce.2.cloned.1.call-start = ((), (), s32[]{:S(2)}) async-start(), calls=%async_computation.5 | async-start | bytes 5242880 | tf_op jit(solution)/shard_map/psum | solution.py:137
  226.9 73.8 %copy-start.1 = (bf16[1,256,5120]{2,1,0:T(8,128)(2,1)S(1)}, bf16[1,256,5120]{2,1,0:T(8,128)(2,1)}, u32[]{:S(2)}) copy-start(bf16[1,256,5120]{2,1,0:T(8,128)(2,1)} %all-gather.6.cloned.1.call-done) | copy-start | bytes 7864324
  232.7 72.5 %copy-start.12 = (f32[5120]{0:T(1024)S(1)}, f32[5120]{0:T(1024)}, u32[]{:S(2)}) copy-start(f32[5120]{0:T(1024)} %param.20) | copy-start | bytes 61444
  232.7 146.6 %reduce-scatter.2.cloned.1.call-start = ((), (), s32[]{:S(2)}) async-start(), calls=%async_computation.6 | async-start | bytes 2949120 | tf_op jit(solution)/shard_map/reduce_scatter | solution.py:144
  303.7 1.5 copy-start.2
  314.1 28.5 %copy-start.11 = (bf16[32,8,128]{2,0,1:T(8,128)(2,1)S(1)}, bf16[32,8,128]{2,0,1:T(8,128)(2,1)}, u32[]{:S(2)}) copy-start(bf16[32,8,128]{2,0,1:T(8,128)(2,1)} %copy-done.10) | copy-start | bytes 196612
Sparse Core Ops, SparseCore 0:
  9.6 36.5 all-gather.5
  55.9 37.2 all-gather.3
  232.8 67.8 all-reduce.1
  342.7 36.5 reduce-scatter.1
